TPU v7x, 32 devices: a whole 2x2x4 slice. The times are simulated.
32 devices in a mesh: groups: 2 (over y), seq: 8 (over z, x), head: 2 (over core).
Axes of the slice: x: 2, y: 2, z: 4, core: 2. Of those that a mesh axis runs over, the one named last changes fastest.
Arguments:
- queries: bfloat16 [2048, 1024], P(('groups', 'seq'), 'head'), parts along dimension 0, may hold values from -600 to 600
- keys: bfloat16 [2048, 1024], P(('groups', 'seq'), 'head'), parts along dimension 0, may hold values from -600 to 600
- values: bfloat16 [2048, 1024], P(('groups', 'seq'), 'head'), parts along dimension 0, may hold values from -600 to 600
- out_weight: bfloat16 [2048, 1024], P('seq', 'head'), may hold values from -0.1875 to 0.1875
- grad_y: bfloat16 [2048, 2048], P(('groups', 'seq')), parts along dimension 0, may hold values from -6 to 6
Outputs:
- out_y: bfloat16 [2048, 2048], P(('groups', 'seq')), parts along dimension 0
- grad_queries: bfloat16 [2048, 1024], P(('groups', 'seq'), 'head'), parts along dimension 0
- grad_keys: bfloat16 [2048, 1024], P(('groups', 'seq'), 'head'), parts along dimension 0
- grad_values: bfloat16 [2048, 1024], P(('groups', 'seq'), 'head'), parts along dimension 0
- grad_weight: float32 [4096, 1024], P(('groups', 'seq'), 'head'), parts along dimension 0
There are 2 independent parts, one for each index of `groups`. A program takes and returns all parts, laid end to end along the dimension named above; an argument that names none is the same for every part. Nothing has to cross between parts.
All inputs are finite; a program needn't handle non-finite values.
Results may differ from a plain program's by a relative error of at most 0.009.
Values may be sent and summed in bfloat16 or wider, within the bound.
No kernel may reach another device: no remote copies, remote signals or barrier semaphores. Data moves between devices by JAX's collectives and lax.ppermute only.
A program may use at most 192 MiB of HBM per device.

v0:
```python
import jax
import jax.numpy as jnp
from jax import lax
from jax.sharding import PartitionSpec as P

DH = 128
TILE = 128
epsilon = 1e-06


def carried_in(value, axis, join, neutral, backward):
    count, mine = (lax.axis_size(axis), lax.axis_index(axis))
    pieces = lax.all_gather(value, axis)
    if backward:
        pieces = pieces[::-1]
        mine = count - 1 - mine
    so_far = jnp.full_like(value, 0) + jnp.asarray(neutral, value.dtype)

    def turn(position, so_far):
        longer = join(so_far, pieces[position])
        return jnp.where(position < mine, longer, so_far)

    return lax.fori_loop(0, count - 1, turn, so_far)


def add_states(earlier, later):
    return earlier + later


def on_device(queries, keys, values, out_weight, grad_y):
    row_count = queries.shape[0]
    tile_count = row_count // TILE
    head_count = queries.shape[1] // DH

    def tiled(array):
        return array.reshape(tile_count, TILE, head_count, DH)

    query_tiles = tiled(queries)
    key_tiles = tiled(keys)
    value_tiles = tiled(values)
    causal = lax.broadcasted_iota(jnp.int32, (TILE, TILE), 0) >= lax.broadcasted_iota(
        jnp.int32, (TILE, TILE), 1
    )
    raw_scores = jnp.einsum(
        "nthd,nshd->nhts", query_tiles, key_tiles, preferred_element_type=jnp.float32
    )
    scores = jnp.where(causal, raw_scores, 0.0).astype(jnp.bfloat16)
    states = jnp.einsum(
        "nshd,nshe->nhde", key_tiles, value_tiles, preferred_element_type=jnp.float32
    )
    empty_state = jnp.zeros(states.shape[1:], jnp.float32)
    device_prefix = carried_in(jnp.sum(states, axis=0), "seq", add_states, empty_state, False)
    prefix_state = (device_prefix[None] + (jnp.cumsum(states, axis=0) - states)).astype(
        jnp.bfloat16
    )
    attended = jnp.einsum(
        "nhts,nshe->nthe", scores, value_tiles, preferred_element_type=jnp.float32
    )
    attended = attended + jnp.einsum(
        "nthd,nhde->nthe", query_tiles, prefix_state, preferred_element_type=jnp.float32
    )
    inverse_rms = lax.rsqrt(jnp.mean(attended * attended, axis=-1, keepdims=True) + epsilon)
    normed_exact = attended * inverse_rms
    normed = normed_exact.astype(jnp.bfloat16).reshape(row_count, -1)
    contract_last = (((1,), (1,)), ((), ()))
    back_weight = lax.all_gather(out_weight, "seq", axis=0, tiled=True)
    grad_normed = jnp.dot(grad_y, back_weight, preferred_element_type=jnp.float32)
    fore_weight = lax.all_gather(out_weight, "seq", axis=0, tiled=True)
    partial_out = lax.dot_general(
        normed, fore_weight, contract_last, preferred_element_type=jnp.float32
    )
    out_y = lax.psum(partial_out.astype(jnp.bfloat16), "head")
    grad_tiles = tiled(grad_normed)
    projected = jnp.mean(grad_tiles * normed_exact, axis=-1, keepdims=True)
    grad_out = (inverse_rms * (grad_tiles - normed_exact * projected)).astype(jnp.bfloat16)
    raw_grad = jnp.einsum(
        "nthe,nshe->nhts", grad_out, value_tiles, preferred_element_type=jnp.float32
    )
    grad_scores = jnp.where(causal, raw_grad, 0.0).astype(jnp.bfloat16)
    adjoint = jnp.einsum(
        "nthd,nthe->nhde", query_tiles, grad_out, preferred_element_type=jnp.float32
    )
    own_adjoint = jnp.sum(adjoint, axis=0)
    device_suffix = carried_in(own_adjoint, "seq", add_states, empty_state, True)
    later_tiles = jnp.flip(jnp.cumsum(jnp.flip(adjoint, 0), axis=0), 0) - adjoint
    suffix_state = (device_suffix[None] + later_tiles).astype(jnp.bfloat16)
    grad_queries = jnp.einsum(
        "nhts,nshd->nthd", grad_scores, key_tiles, preferred_element_type=jnp.float32
    )
    grad_queries = grad_queries + jnp.einsum(
        "nthe,nhde->nthd", grad_out, prefix_state, preferred_element_type=jnp.float32
    )
    grad_keys = jnp.einsum(
        "nhts,nthd->nshd", grad_scores, query_tiles, preferred_element_type=jnp.float32
    )
    grad_keys = grad_keys + jnp.einsum(
        "nshe,nhde->nshd", value_tiles, suffix_state, preferred_element_type=jnp.float32
    )
    grad_values = jnp.einsum(
        "nhts,nthe->nshe", scores, grad_out, preferred_element_type=jnp.float32
    )
    grad_values = grad_values + jnp.einsum(
        "nshd,nhde->nshe", key_tiles, suffix_state, preferred_element_type=jnp.float32
    )
    grad_weight = lax.psum_scatter(
        lax.dot_general(
            grad_y, normed, (((0,), (0,)), ((), ())), preferred_element_type=jnp.float32
        ),
        "seq",
        scatter_dimension=0,
        tiled=True,
    )
    return (
        out_y,
        grad_queries.reshape(row_count, -1).astype(jnp.bfloat16),
        grad_keys.reshape(row_count, -1).astype(jnp.bfloat16),
        grad_values.reshape(row_count, -1).astype(jnp.bfloat16),
        grad_weight,
    )


def solution(mesh):
    placed = (
        P(("groups", "seq"), "head"),
        P(("groups", "seq"), "head"),
        P(("groups", "seq"), "head"),
        P("seq", "head"),
        P(("groups", "seq"), None),
    )
    return jax.shard_map(
        on_device,
        mesh=mesh,
        in_specs=placed,
        out_specs=(
            P(("groups", "seq"), None),
            P(("groups", "seq"), "head"),
            P(("groups", "seq"), "head"),
            P(("groups", "seq"), "head"),
            P(("groups", "seq"), "head"),
        ),
        check_vma=False,
    )
```

profile of v0, /device:TPU:0, one launch (start us, length us, event | category | flops | bytes accessed | tf_op | source)
XLA Modules:
  0.0 284.6 jit_solution(14528810327368836696)
XLA Ops:
  7.2 1.1 copy.104
  8.3 1.8 fusion.10
  11.0 1.2 fusion.1
  12.8 1.1 convolution_bitcast_fusion.4
  14.0 48.7 %all-gather.8.cloned.1.call-done = f32[32,128,128]{2,1,0:T(8,128)} async-done(((f32[4,128,128]{2,1,0:T(8,128)}), f32[32,128,128]{2,1,0:T(8,128)}) %all-gather.8.cloned.1.call-update) | async-done | bytes 2097168 | tf_op jit(solution)/shard_map/all_gather | solution.py:13
  62.7 7.5 %while.28 = (s32[]{:T(128)}, f32[4,128,128]{2,1,0:T(8,128)S(1)}, s32[]{:T(128)}, f32[8,4,128,128]{3,2,1,0:T(8,128)}, s32[]{:T(128)}, /*index=5*/s32[]{:T(128)}) while((s32[]{:T(128)}, f32[4,128,128]{2,1,0:T(8,128)S(1)}, s32[]{:T(128)}, f32[8,4,128,128]{3,2,1,0:T(8,128)}, s32[]{:T(128)}, /*index=5*/s32[]{:T(128)}) %tuple.84), condition=%wide.region_1.2_spmd.clone, body=%wide.region_0.1_spmd.clone.sunk | while | flops 196612 | bytes 786533 | solution.py:23
  62.7 1.1 add_select_fusion.4
  68.1 1.0 add_select_fusion.4
  69.2 1.0 add_select_fusion.4
  70.5 42.1 %all-gather.6.cloned.1.call-done = bf16[2048,512]{1,0:T(8,128)(2,1)} async-done(((bf16[256,512]{1,0:T(8,128)(2,1)}), bf16[2048,512]{1,0:T(8,128)(2,1)}) %all-gather.6.cloned.1.call-update) | async-done | bytes 2097168 | tf_op jit(solution)/shard_map/all_gather | solution.py:68
  112.7 2.5 fusion.28
  116.4 2.7 convolution_bitcast_fusion
  120.2 1.2 convolution_bitcast_fusion.3
  122.2 1.7 copy.52
  123.9 1.9 convolution_bitcast_fusion.1
  125.8 1.8 fusion.29
  127.6 2.5 convolution_convert_fusion
  130.2 34.2 %all-gather.10.cloned.1.call-done = f32[32,128,128]{2,1,0:T(8,128)} async-done(((f32[4,128,128]{2,1,0:T(8,128)}), f32[32,128,128]{2,1,0:T(8,128)}) %all-gather.10.cloned.1.call-update) | async-done | bytes 2097168 | tf_op jit(solution)/shard_map/all_gather | solution.py:13
  164.3 1.7 rev.3
  167.1 1.2 fusion.4
  170.0 84.8 %reduce-scatter.2.cloned.1.call-done = f32[256,512]{0,1:T(8,128)} async-done(((f32[2048,512]{0,1:T(8,128)}), f32[256,512]{0,1:T(8,128)}) %reduce-scatter.2.cloned.1.call-update) | async-done | bytes 524304 | tf_op jit(solution)/shard_map/reduce_scatter | solution.py:105
  254.8 2.0 copy.55
  256.8 19.4 %all-reduce.2.cloned.1.call-done = bf16[128,2048]{1,0:T(8,128)(2,1)} async-done(((bf16[128,2048]{1,0:T(8,128)(2,1)}), bf16[128,2048]{1,0:T(8,128)(2,1)}) %all-reduce.2.cloned.1.call-update) | async-done | bytes 524304 | tf_op jit(solution)/shard_map/psum | solution.py:72
  276.2 1.9 copy.120
  (62 shorter events, 12.4 us)
Async XLA Ops:
  7.2 105.5 %copy-start = (bf16[128,2048]{1,0:T(8,128)(2,1)S(1)}, bf16[128,2048]{1,0:T(8,128)(2,1)}, u32[]{:S(2)}) copy-start(bf16[128,2048]{1,0:T(8,128)(2,1)} %param.13) | copy-start | bytes 1572868
  7.2 55.6 %all-gather.8.cloned.1.call-start = ((), (), s32[]{:S(2)}) async-start(), calls=%async_computation.4 | async-start | bytes 2359296 | tf_op jit(solution)/shard_map/all_gather | solution.py:13
  8.3 2.6 copy-start.4
  10.2 102.5 %all-gather.6.cloned.1.call-start = ((), (), s32[]{:S(2)}) async-start(), calls=%async_computation.1 | async-start | bytes 2359296 | tf_op jit(solution)/shard_map/all_gather | solution.py:68
  10.9 153.4 %all-gather.10.cloned.1.call-start = ((), (), s32[]{:S(2)}) async-start(), calls=%async_computation.5 | async-start | bytes 2359296 | tf_op jit(solution)/shard_map/all_gather | solution.py:13
  12.2 0.6 copy-start.9
  14.0 56.2 %copy-start.2 = (f32[4,128,128]{2,1,0:T(8,128)S(1)}, f32[4,128,128]{2,1,0:T(8,128)}, u32[]{:S(2)}) copy-start(f32[4,128,128]{2,1,0:T(8,128)} %fusion.10) | copy-start | bytes 786436
  62.7 7.5 %copy-start.5 = (bf16[128,512]{1,0:T(8,128)(2,1)S(1)}, bf16[128,512]{1,0:T(8,128)(2,1)}, u32[]{:S(2)}) copy-start(bf16[128,512]{1,0:T(8,128)(2,1)} %param.9) | copy-start | bytes 393220
  115.3 3.7 %copy-start.6 = (bf16[1,128,4,128]{1,3,2,0:T(8,128)(2,1)}, bf16[1,128,4,128]{1,3,2,0:T(8,128)(2,1)S(1)}, u32[]{:S(2)}) copy-start(bf16[1,128,4,128]{1,3,2,0:T(8,128)(2,1)S(1)} %get-tuple-element.222) | copy-start | bytes 393220
  116.4 138.5 %reduce-scatter.2.cloned.1.call-start = ((), (), s32[]{:S(2)}) async-start(), calls=%async_computation.3 | async-start | bytes 4718592 | tf_op jit(solution)/shard_map/reduce_scatter | solution.py:105
  119.1 0.9 copy-start.3
  119.1 8.5 %copy-start.1 = (bf16[2048,512]{1,0:T(8,128)(2,1)S(1)}, bf16[2048,512]{1,0:T(8,128)(2,1)}, u32[]{:S(2)}) copy-start(bf16[2048,512]{1,0:T(8,128)(2,1)} %all-gather.6.cloned.1.call-done) | copy-start | bytes 6291460
  119.1 157.1 %all-reduce.2.cloned.1.call-start = ((), (), s32[]{:S(2)}) async-start(), calls=%async_computation.2 | async-start | bytes 1048576 | tf_op jit(solution)/shard_map/psum | solution.py:72
  120.2 2.0 copy-start.10
  166.1 2.9 %copy-start.7 = (f32[4,128,128]{2,1,0:T(8,128)S(1)}, f32[4,128,128]{2,1,0:T(8,128)}, u32[]{:S(2)}) copy-start(f32[4,128,128]{2,1,0:T(8,128)} %fusion.29) | copy-start | bytes 786436
  166.9 2.2 copy-start.8
Sparse Core Ops, SparseCore 0:
  10.7 51.9 all-gather.7
  64.9 47.7 all-gather.5
  116.5 47.8 all-gather.9
  167.8 86.9 reduce-scatter.1
  257.7 18.4 all-reduce.1
where the time goes:
time: 285 us
  waiting for transfers between devices  230 us (81%)
  matrix products  19.6 us (7%)
  between operations  14 us (5%)
  local copies, waits for them, and re-layouts  12.4 us (4%)
  other arithmetic  8.1 us (3%)
    reduce_scatter x1, waiting for transfers between devices, on_device(): lax.psum_scatter(lax.dot_general(grad_y, normed, (((0,), (0,)), ((), ()))...  84.8 us
    all_gather x2, waiting for transfers between devices, carried_in(): pieces = lax.all_gather(value, axis)  82.9 us
    all_gather x1, waiting for transfers between devices, on_device(): fore_weight = lax.all_gather(out_weight, 'seq', axis=0, tiled=True)  42.1 us
    psum x1, waiting for transfers between devices, on_device(): out_y = lax.psum(partial_out.astype(jnp.bfloat16), 'head')  19.4 us
    unnamed x27, local copies, waits for them, and re-layouts  8.63 us
    select_n x14, other arithmetic, turn(): return jnp.where(position < mine, longer, so_far)  7.89 us
  transfers between devices with their start and end apart: 5, of which 5 were waited for; matrix products, arithmetic and copies ran while one was open for 11% of the time, Pallas kernels for 0%

commit v1 on v0

--- a/solution.py
+++ b/solution.py
@@ -65,7 +65,25 @@
     contract_last = (((1,), (1,)), ((), ()))
     back_weight = lax.all_gather(out_weight, "seq", axis=0, tiled=True)
     grad_normed = jnp.dot(grad_y, back_weight, preferred_element_type=jnp.float32)
-    fore_weight = lax.all_gather(out_weight, "seq", axis=0, tiled=True)
+    peers, index, rows = (lax.axis_size("seq"), lax.axis_index("seq"), out_weight.shape[0])
+    right = [(i, (i + 1) % peers) for i in range(peers)]
+    behind = [(i, (i - 1) % peers) for i in range(peers)]
+    fore_weight = jnp.zeros(
+        (*out_weight.shape[:0], peers * rows, *out_weight.shape[0 + 1 :]), out_weight.dtype
+    )
+    fore_weight = lax.dynamic_update_slice_in_dim(fore_weight, out_weight, index * rows, axis=0)
+    from_left = from_right = out_weight
+    half = peers // 2
+    for step in range(1, half + 1):
+        from_left = lax.ppermute(from_left, "seq", right)
+        fore_weight = lax.dynamic_update_slice_in_dim(
+            fore_weight, from_left, (index - step) % peers * rows, axis=0
+        )
+        if step < peers - half:
+            from_right = lax.ppermute(from_right, "seq", behind)
+            fore_weight = lax.dynamic_update_slice_in_dim(
+                fore_weight, from_right, (index + step) % peers * rows, axis=0
+            )
     partial_out = lax.dot_general(
         normed, fore_weight, contract_last, preferred_element_type=jnp.float32
     )

time: 285 us -> 308 us (1.081)
  starting transfers between devices: 0.2 us -> 15.4 us
  waiting for transfers between devices: 230 us -> 235 us
  local copies, waits for them, and re-layouts: 12.4 us -> 15.9 us
    ppermute x0 -> x7, waiting for transfers between devices: none -> 39.7 us  [the longest x4 37.8 us: on_device(): from_left = lax.ppermute(from_left, 'seq', right)]
    all_gather x2, waiting for transfers between devices: 82.9 us -> 49.3 us  [carried_in(): pieces = lax.all_gather(value, axis)]
    ppermute x0 -> x7, starting transfers between devices: none -> 15.2 us  [the longest x4 8 us: on_device(): from_left = lax.ppermute(from_left, 'seq', right)]
    dynamic_update_slice x0 -> x8, local copies, waits for them, and re-layouts: none -> 3.97 us  [the longest x4 1.98 us: on_device(): lax.dynamic_update_slice_in_dim(fore_weight, from_left, (index - step) %...]
    unnamed x27 -> x29, local copies, waits for them, and re-layouts: 8.63 us -> 8.06 us
  transfers between devices with their start and end apart: 5 -> 12, of which waited for: 5 -> 9; matrix products, arithmetic and copies ran while one was open for 11% -> 11% of each run, Pallas kernels for 0% -> 0%
where the time goes in v1:
time: 308 us; the launch traced here: 307 us
  waiting for transfers between devices  235 us (76%)
  matrix products  18.6 us (6%)
  local copies, waits for them, and re-layouts  15.9 us (5%)
  starting transfers between devices  15.4 us (5%)
  between operations  14.3 us (5%)
  other arithmetic  8.11 us (3%)
    reduce_scatter x1, waiting for transfers between devices, on_device(): lax.psum_scatter(lax.dot_general(grad_y, normed, (((0,), (0,)), ((), ()))...  83.4 us
    all_gather x2, waiting for transfers between devices, carried_in(): pieces = lax.all_gather(value, axis)  49.3 us
    all_gather x1, waiting for transfers between devices, on_device(): back_weight = lax.all_gather(out_weight, 'seq', axis=0, tiled=True)  42.1 us
    ppermute x4, waiting for transfers between devices, on_device(): from_left = lax.ppermute(from_left, 'seq', right)  37.8 us
    psum x1, waiting for transfers between devices, on_device(): out_y = lax.psum(partial_out.astype(jnp.bfloat16), 'head')  19.4 us
    unnamed x29, local copies, waits for them, and re-layouts  8.06 us
    ppermute x4, starting transfers between devices, on_device(): from_left = lax.ppermute(from_left, 'seq', right)  8 us
    select_n x14, other arithmetic, turn(): return jnp.where(position < mine, longer, so_far)  7.89 us
  transfers between devices with their start and end apart: 12, of which 9 were waited for; matrix products, arithmetic and copies ran while one was open for 11% of the time, Pallas kernels for 0%

profile of v1, /device:TPU:0, one launch (start us, length us, event | category | flops | bytes accessed | tf_op | source)
XLA Modules:
  0.0 307.4 jit_solution(10749797592657395628)
XLA Ops:
  8.3 1.8 fusion.10
  13.4 49.3 %all-gather.8.cloned.1.call-done = f32[32,128,128]{2,1,0:T(8,128)} async-done(((f32[4,128,128]{2,1,0:T(8,128)}), f32[32,128,128]{2,1,0:T(8,128)}) %all-gather.8.cloned.1.call-update) | async-done | bytes 2097168 | tf_op jit(solution)/shard_map/all_gather | solution.py:13
  62.7 7.5 %while.28 = (s32[]{:T(128)}, f32[4,128,128]{2,1,0:T(8,128)S(1)}, s32[]{:T(128)}, f32[8,4,128,128]{3,2,1,0:T(8,128)}, s32[]{:T(128)}, /*index=5*/s32[]{:T(128)}) while((s32[]{:T(128)}, f32[4,128,128]{2,1,0:T(8,128)S(1)}, s32[]{:T(128)}, f32[8,4,128,128]{3,2,1,0:T(8,128)}, s32[]{:T(128)}, /*index=5*/s32[]{:T(128)}) %tuple.84), condition=%wide.region_1.2_spmd.clone, body=%wide.region_0.1_spmd.clone.sunk | while | flops 196612 | bytes 786525 | solution.py:23
  70.5 42.1 %all-gather.6.cloned.1.call-done = bf16[2048,512]{1,0:T(8,128)(2,1)} async-done(((bf16[256,512]{1,0:T(8,128)(2,1)}), bf16[2048,512]{1,0:T(8,128)(2,1)}) %all-gather.6.cloned.1.call-update) | async-done | bytes 2097168 | tf_op jit(solution)/shard_map/all_gather | solution.py:66
  112.7 2.5 fusion.28
  116.4 2.6 convolution_bitcast_fusion
  120.6 4.2 %collective-permute-start.1 = (bf16[256,512]{1,0:T(8,128)(2,1)S(1)}, bf16[256,512]{1,0:T(8,128)(2,1)}, u32[]{:S(2)}, u32[]{:S(2)}) collective-permute-start(bf16[256,512]{1,0:T(8,128)(2,1)S(1)} %copy-done.7), channel_id=1, source_target_pairs={{0,14},{2,0},{4,2},{6,4},{8,6},{10,8},{12,10},{14,12},{1,15},{3,1}... | collective-permute-start | bytes 786440 | tf_op jit(solution)/shard_map/ppermute | solution.py:83
  124.7 10.2 %collective-permute-done = bf16[256,512]{1,0:T(8,128)(2,1)} collective-permute-done((bf16[256,512]{1,0:T(8,128)(2,1)S(1)}, bf16[256,512]{1,0:T(8,128)(2,1)}, u32[]{:S(2)}, u32[]{:S(2)}) %collective-permute-start) | collective-permute-done | bytes 262176 | tf_op jit(solution)/shard_map/ppermute | solution.py:78
  135.0 2.6 collective-permute-start.2
  137.6 1.9 collective-permute-done.1
  140.6 8.5 %collective-permute-done.2 = bf16[256,512]{1,0:T(8,128)(2,1)} collective-permute-done((bf16[256,512]{1,0:T(8,128)(2,1)}, bf16[256,512]{1,0:T(8,128)(2,1)}, u32[]{:S(2)}, u32[]{:S(2)}) %collective-permute-start.2) | collective-permute-done | bytes 262176 | tf_op jit(solution)/shard_map/ppermute | solution.py:78
  149.1 2.5 collective-permute-start.4
  153.6 2.3 collective-permute-start.5
  156.9 12.7 %collective-permute-done.4 = bf16[256,512]{1,0:T(8,128)(2,1)S(1)} collective-permute-done((bf16[256,512]{1,0:T(8,128)(2,1)}, bf16[256,512]{1,0:T(8,128)(2,1)S(1)}, u32[]{:S(2)}, u32[]{:S(2)}) %collective-permute-start.4) | collective-permute-done | bytes 262176 | tf_op jit(solution)/shard_map/ppermute | solution.py:78
  169.5 2.4 collective-permute-start.6
  172.9 6.3 %collective-permute-done.6 = bf16[256,512]{1,0:T(8,128)(2,1)S(1)} collective-permute-done((bf16[256,512]{1,0:T(8,128)(2,1)S(1)}, bf16[256,512]{1,0:T(8,128)(2,1)S(1)}, u32[]{:S(2)}, u32[]{:S(2)}) %collective-permute-start.6) | collective-permute-done | bytes 262176 | tf_op jit(solution)/shard_map/ppermute | solution.py:78
  182.3 1.9 convolution_bitcast_fusion.1
  184.2 1.8 fusion.29
  186.0 2.5 convolution_convert_fusion
  188.5 1.7 rev.3
  194.2 83.4 %reduce-scatter.2.cloned.1.call-done = f32[256,512]{0,1:T(8,128)} async-done(((f32[2048,512]{0,1:T(8,128)}), f32[256,512]{0,1:T(8,128)}) %reduce-scatter.2.cloned.1.call-update) | async-done | bytes 524304 | tf_op jit(solution)/shard_map/reduce_scatter | solution.py:123
  277.6 2.0 copy.55
  279.7 19.4 %all-reduce.2.cloned.1.call-done = bf16[128,2048]{1,0:T(8,128)(2,1)} async-done(((bf16[128,2048]{1,0:T(8,128)(2,1)}), bf16[128,2048]{1,0:T(8,128)(2,1)}) %all-reduce.2.cloned.1.call-update) | async-done | bytes 524304 | tf_op jit(solution)/shard_map/psum | solution.py:90
  299.0 1.9 copy.128
  (87 shorter events, 26.9 us)
Async XLA Ops:
  7.2 105.5 %copy-start = (bf16[128,2048]{1,0:T(8,128)(2,1)S(1)}, bf16[128,2048]{1,0:T(8,128)(2,1)}, u32[]{:S(2)}) copy-start(bf16[128,2048]{1,0:T(8,128)(2,1)} %param.13) | copy-start | bytes 1572868
  7.2 55.6 %all-gather.8.cloned.1.call-start = ((), (), s32[]{:S(2)}) async-start(), calls=%async_computation.4 | async-start | bytes 2359296 | tf_op jit(solution)/shard_map/all_gather | solution.py:13
  8.3 2.7 copy-start.3
  10.2 102.5 %all-gather.6.cloned.1.call-start = ((), (), s32[]{:S(2)}) async-start(), calls=%async_computation.2 | async-start | bytes 2359296 | tf_op jit(solution)/shard_map/all_gather | solution.py:66
  10.9 177.6 %all-gather.10.cloned.1.call-start = ((), (), s32[]{:S(2)}) async-start(), calls=%async_computation.5 | async-start | bytes 2359296 | tf_op jit(solution)/shard_map/all_gather | solution.py:13
  12.2 50.5 %copy-start.10 = (bf16[4,128,128]{2,1,0:T(8,128)(2,1)}, bf16[4,128,128]{2,1,0:T(8,128)(2,1)S(1)}, u32[]{:S(2)}) copy-start(bf16[4,128,128]{2,1,0:T(8,128)(2,1)S(1)} %fusion.1) | copy-start | bytes 393220
  13.4 56.8 %copy-start.1 = (f32[4,128,128]{2,1,0:T(8,128)S(1)}, f32[4,128,128]{2,1,0:T(8,128)}, u32[]{:S(2)}) copy-start(f32[4,128,128]{2,1,0:T(8,128)} %fusion.10) | copy-start | bytes 786436
  62.7 7.5 %copy-start.5 = (bf16[128,512]{1,0:T(8,128)(2,1)S(1)}, bf16[128,512]{1,0:T(8,128)(2,1)}, u32[]{:S(2)}) copy-start(bf16[128,512]{1,0:T(8,128)(2,1)} %param.9) | copy-start | bytes 393220
  115.3 3.7 %copy-start.6 = (bf16[1,128,4,128]{1,3,2,0:T(8,128)(2,1)}, bf16[1,128,4,128]{1,3,2,0:T(8,128)(2,1)S(1)}, u32[]{:S(2)}) copy-start(bf16[1,128,4,128]{1,3,2,0:T(8,128)(2,1)S(1)} %get-tuple-element.222) | copy-start | bytes 393220
  116.4 161.3 %reduce-scatter.2.cloned.1.call-start = ((), (), s32[]{:S(2)}) async-start(), calls=%async_computation.3 | async-start | bytes 4718592 | tf_op jit(solution)/shard_map/reduce_scatter | solution.py:123
  119.1 1.0 copy-start.7
  119.1 179.9 %all-reduce.2.cloned.1.call-start = ((), (), s32[]{:S(2)}) async-start(), calls=%async_computation.1 | async-start | bytes 1048576 | tf_op jit(solution)/shard_map/psum | solution.py:90
  120.0 15.0 %collective-permute-start = (bf16[256,512]{1,0:T(8,128)(2,1)S(1)}, bf16[256,512]{1,0:T(8,128)(2,1)}, u32[]{:S(2)}, u32[]{:S(2)}) collective-permute-start(bf16[256,512]{1,0:T(8,128)(2,1)S(1)} %copy-done.7), channel_id=1, source_target_pairs={{0,2},{2,4},{4,6},{6,8},{8,10},{10,12},{12,14},{14,0},{1,3},{3,5},... | collective-permute-start | bytes 786440 | tf_op jit(solution)/shard_map/ppermute | solution.py:78
  120.6 18.9 %collective-permute-start.1 = (bf16[256,512]{1,0:T(8,128)(2,1)S(1)}, bf16[256,512]{1,0:T(8,128)(2,1)}, u32[]{:S(2)}, u32[]{:S(2)}) collective-permute-start(bf16[256,512]{1,0:T(8,128)(2,1)S(1)} %copy-done.7), channel_id=1, source_target_pairs={{0,14},{2,0},{4,2},{6,4},{8,6},{10,8},{12,10},{14,12},{1,15},{3,1}... | collective-permute-start | bytes 786440 | tf_op jit(solution)/shard_map/ppermute | solution.py:83
  135.0 14.2 %collective-permute-start.2 = (bf16[256,512]{1,0:T(8,128)(2,1)}, bf16[256,512]{1,0:T(8,128)(2,1)}, u32[]{:S(2)}, u32[]{:S(2)}) collective-permute-start(bf16[256,512]{1,0:T(8,128)(2,1)} %collective-permute-done), channel_id=1, source_target_pairs={{0,2},{2,4},{4,6},{6,8},{8,10},{10,12},{12,14},{14,0},{1,3},{3,5},... | collective-permute-start | bytes 786440 | tf_op jit(solution)/shard_map/ppermute | solution.py:78
  139.5 14.1 %collective-permute-start.3 = (bf16[256,512]{1,0:T(8,128)(2,1)}, bf16[256,512]{1,0:T(8,128)(2,1)}, u32[]{:S(2)}, u32[]{:S(2)}) collective-permute-start(bf16[256,512]{1,0:T(8,128)(2,1)} %collective-permute-done.1), channel_id=1, source_target_pairs={{0,14},{2,0},{4,2},{6,4},{8,6},{10,8},{12,10},{14,12},{1,15},{3,1}... | collective-permute-start | bytes 786440 | tf_op jit(solution)/shard_map/ppermute | solution.py:83
  140.4 38.9 %copy-start.2 = (bf16[128,512]{1,0:T(8,128)(2,1)S(1)}, bf16[128,512]{1,0:T(8,128)(2,1)}, u32[]{:S(2)}) copy-start(bf16[128,512]{1,0:T(8,128)(2,1)} %param.11) | copy-start | bytes 393220
  140.6 39.0 %copy-start.4 = (bf16[128,512]{0,1:T(8,128)(2,1)S(1)}, bf16[128,512]{0,1:T(8,128)(2,1)}, u32[]{:S(2)}) copy-start(bf16[128,512]{0,1:T(8,128)(2,1)} %copy-done.3) | copy-start | bytes 393220
  149.1 20.4 %collective-permute-start.4 = (bf16[256,512]{1,0:T(8,128)(2,1)}, bf16[256,512]{1,0:T(8,128)(2,1)S(1)}, u32[]{:S(2)}, u32[]{:S(2)}) collective-permute-start(bf16[256,512]{1,0:T(8,128)(2,1)} %collective-permute-done.2), channel_id=1, source_target_pairs={{0,2},{2,4},{4,6},{6,8},{8,10},{10,12},{12,14},{14,0},{1,3},{3,5},... | collective-permute-start | bytes 786440 | tf_op jit(solution)/shard_map/ppermute | solution.py:78
  153.6 19.3 %collective-permute-start.5 = (bf16[256,512]{1,0:T(8,128)(2,1)}, bf16[256,512]{1,0:T(8,128)(2,1)S(1)}, u32[]{:S(2)}, u32[]{:S(2)}) collective-permute-start(bf16[256,512]{1,0:T(8,128)(2,1)} %collective-permute-done.3), channel_id=1, source_target_pairs={{0,14},{2,0},{4,2},{6,4},{8,6},{10,8},{12,10},{14,12},{1,15},{3,1}... | collective-permute-start | bytes 786440 | tf_op jit(solution)/shard_map/ppermute | solution.py:83
  169.5 9.7 %collective-permute-start.6 = (bf16[256,512]{1,0:T(8,128)(2,1)S(1)}, bf16[256,512]{1,0:T(8,128)(2,1)S(1)}, u32[]{:S(2)}, u32[]{:S(2)}) collective-permute-start(bf16[256,512]{1,0:T(8,128)(2,1)S(1)} %collective-permute-done.4), channel_id=1, source_target_pairs={{0,2},{2,4},{4,6},{6,8},{8,10},{10,12},{12,14},{14,0},{1,3},{3,5},... | collective-permute-start | bytes 786440 | tf_op jit(solution)/shard_map/ppermute | solution.py:78
  179.6 1.1 copy-start.11
  190.3 2.9 copy-start.9
  191.1 2.2 copy-start.8
Sparse Core Ops, SparseCore 0:
  10.7 51.9 all-gather.7
  64.9 47.7 all-gather.5
  116.5 67.7 all-gather.9
  187.8 89.7 reduce-scatter.1
  280.5 18.4 all-reduce.1
